TPU v7x, 512 devices: a whole 4x8x8 slice. The times are simulated.
512 devices in a mesh: depth: 64 (over z, y), strip: 8 (over x, core).
Axes of the slice: x: 4, y: 8, z: 8, core: 2. Of those that a mesh axis runs over, the one named last changes fastest.
Arguments:
- volume: float32 [128, 512, 1024], P('strip', 'depth'), may hold values from -4.5 to 6.5
- extinction: float32 [1], replicated, may hold values from 0.0005859375 to 0.001953125
- color_map: float32 [3, 2], replicated, may hold values from -3 to 3
- light_direction: float32 [3], replicated, may hold values from -4 to 4
Outputs:
- image: float32 [4, 128, 1024], P(None, 'strip', 'depth')
All inputs are finite; a program needn't handle non-finite values.
Results may differ from a plain program's by a relative error of at most 0.000034.
Values sent between devices are 32-bit elements; how exact they have to be, the bound alone decides.
No kernel may reach another device: no remote copies, remote signals or barrier semaphores. Data moves between devices by JAX's collectives and lax.ppermute only.
A program may use at most 64 MiB of HBM per device.

v0:
```python
import jax
import jax.numpy as jnp
from jax import lax
from jax.sharding import PartitionSpec as P


def extended_2(block, sides, width):
    for axis, dim in sides:
        count = lax.axis_size(axis)
        forward = [(i, i + 1) for i in range(count - 1)]
        backward = [(target, source) for source, target in forward]
        low = lax.ppermute(
            lax.slice_in_dim(block, block.shape[dim] - width, None, axis=dim), axis, forward
        )
        high = lax.ppermute(lax.slice_in_dim(block, 0, width, axis=dim), axis, backward)
        block = jnp.concatenate([low, block, high], axis=dim)
    return block


def blur_valid(field_in, along):
    extent = field_in.shape[along]
    lower_cells = lax.slice_in_dim(field_in, 0, extent - 2, axis=along)
    middle = lax.slice_in_dim(field_in, 1, extent - 1, axis=along)
    upper_cells = lax.slice_in_dim(field_in, 2, extent, axis=along)
    return 0.25 * lower_cells + 0.5 * middle + 0.25 * upper_cells


def slope_valid(field_in, along):
    extent = field_in.shape[along]
    lower_cells = lax.slice_in_dim(field_in, 0, extent - 2, axis=along)
    upper_cells = lax.slice_in_dim(field_in, 2, extent, axis=along)
    return 0.5 * (upper_cells - lower_cells)


def smooth_all(padded):
    return blur_valid(blur_valid(blur_valid(padded, 0), 1), 2)


def gradients(padded):
    first = blur_valid(blur_valid(slope_valid(padded, 0), 1), 2)
    second = blur_valid(blur_valid(slope_valid(padded, 1), 0), 2)
    third = blur_valid(blur_valid(slope_valid(padded, 2), 0), 1)
    return (first, second, third)


def pad_columns(field_in):
    return jnp.pad(field_in, ((0, 0), (0, 0), (1, 1)))


def render_slab(smoothed, gradient, extinction, color_map, light_direction):
    facing = (
        gradient[0] * light_direction[0]
        + gradient[1] * light_direction[1]
        + gradient[2] * light_direction[2]
    )
    shading = 0.3 + 0.7 * facing * facing / (1.0 + facing * facing)
    optical = extinction[0] * jax.nn.softplus(2.0 * smoothed)
    opacity = 1.0 - jnp.exp(-optical)
    prior_depth = jnp.cumsum(optical, axis=1) - optical
    weights = jnp.exp(-prior_depth) * opacity * shading
    colors = jnp.stack(
        [
            jnp.sum(
                weights * jax.nn.sigmoid(color_map[channel, 0] * smoothed + color_map[channel, 1]),
                axis=1,
            )
            for channel in range(3)
        ],
        0,
    )
    transmit = jnp.exp(-jnp.sum(optical, axis=1))
    return jnp.concatenate([colors, transmit[None]], 0)


def local(volume, extinction, color_map, light_direction):
    row_count, slab_count, column_count = volume.shape
    groups = lax.axis_size("depth")
    extended = extended_2(volume, (("depth", 1), ("strip", 0)), 2)
    filtered = smooth_all(pad_columns(extended))
    row_global = lax.axis_index("strip") * row_count + jnp.arange(row_count + 2) - 1
    slab_global = lax.axis_index("depth") * slab_count + jnp.arange(slab_count + 2) - 1
    row_inside = (row_global >= 0) & (row_global < row_count * lax.axis_size("strip"))
    slab_inside = (slab_global >= 0) & (slab_global < slab_count * groups)
    inside = (row_inside[:, None] & slab_inside[None, :]).astype(jnp.float32)
    filtered = filtered * inside[:, :, None]
    smoothed = filtered[1:-1, 1:-1]
    gradient = gradients(pad_columns(filtered))
    partial_value = render_slab(smoothed, gradient, extinction, color_map, light_direction)
    layers = lax.all_to_all(
        partial_value[:, :, None, :], "depth", split_axis=3, concat_axis=2, tiled=True
    )
    through = jnp.cumprod(layers[3], axis=1)
    prior_pass = jnp.concatenate([jnp.ones_like(through[:, :1]), through[:, :-1]], 1)
    colors = jnp.sum(prior_pass[None] * layers[:3], axis=2)
    transmit = through[:, -1]
    return jnp.concatenate([colors, 1.0 - transmit[None]], 0)


def solution(mesh):
    in_specs = (P("strip", "depth", None), P(), P(), P())
    out_specs = P(None, "strip", "depth")
    return jax.shard_map(local, mesh=mesh, in_specs=in_specs, out_specs=out_specs, check_vma=False)
```

profile of v0, /device:TPU:3, one launch (start us, length us, event | category | flops | bytes accessed | tf_op | source)
XLA Modules:
  0.0 90.2 jit_solution(13778293491945401389)
XLA Ops:
  0.0 1.4 %fusion.38 = (f32[16,2,1024]{2,1,0:T(2,128)S(1)}, f32[16,2,1024]{2,1,0:T(2,128)S(1)}) fusion(f32[16,8,1024]{2,1,0:T(8,128)} %param.4), kind=kLoop, calls=%fused_computation.92 | loop fusion | bytes 524288 | tf_op jit(solution)/shard_map/slice | solution.py:13
  1.4 3.2 %collective-permute-start = (f32[16,2,1024]{2,1,0:T(2,128)S(1)}, f32[16,2,1024]{2,1,0:T(2,128)S(1)}, u32[]{:S(2)}, u32[]{:S(2)}) collective-permute-start(f32[16,2,1024]{2,1,0:T(2,128)S(1)} %get-tuple-element.12), channel_id=1, source_target_pairs={{0,8},{8,16},{16,24},{24,32},{32,40},{40,48},{48,56},{56,64},{64,7... | collective-permute-start | bytes 393224 | tf_op jit(solution)/shard_map/ppermute | solution.py:12
  4.6 1.3 %collective-permute-start.1 = (f32[16,2,1024]{2,1,0:T(2,128)S(1)}, f32[16,2,1024]{2,1,0:T(2,128)S(1)}, u32[]{:S(2)}, u32[]{:S(2)}) collective-permute-start(f32[16,2,1024]{2,1,0:T(2,128)S(1)} %get-tuple-element.13), channel_id=1, source_target_pairs={{8,0},{16,8},{24,16},{32,24},{40,32},{48,40},{56,48},{64,56},{72,6... | collective-permute-start | bytes 393224 | tf_op jit(solution)/shard_map/ppermute | solution.py:15
  6.7 1.6 %fusion.39 = (f32[1,1]{0,1:T(1,128)}, f32[1,1]{0,1:T(1,128)}, f32[1,1]{0,1:T(1,128)}, f32[1,1]{0,1:T(1,128)}, f32[1,1]{0,1:T(1,128)}, /*index=5*/f32[1,1]{0,1:T(1,128)}) fusion(f32[3,2]{0,1:T(2,128)} %param.6), kind=kLoop, calls=%fused_computation.93 | loop fusion | bytes 48 | tf_op jit(solution)/shard_map/slice | solution.py:64
  8.2 2.1 %collective-permute-done.1 = f32[16,2,1024]{2,1,0:T(2,128)S(1)} collective-permute-done((f32[16,2,1024]{2,1,0:T(2,128)S(1)}, f32[16,2,1024]{2,1,0:T(2,128)S(1)}, u32[]{:S(2)}, u32[]{:S(2)}) %collective-permute-start.1) | collective-permute-done | bytes 131104 | tf_op jit(solution)/shard_map/ppermute | solution.py:15
  10.3 0.9 %pad_maximum_fusion.3 = (f32[2,12,1024]{2,1,0:T(8,128)S(1)}, f32[2,12,1024]{2,1,0:T(8,128)S(1)}) fusion(f32[16,2,1024]{2,1,0:T(2,128)S(1)} %collective-permute-done.1, f32[16,8,1024]{2,1,0:T(8,128)} %param.4, f32[16,2,1024]{2,1,0:T(2,128)S(1)} %collective-permute-done), kind=kLoop, calls=%fused_computation.83 | loop fusion | flops 98304 | bytes 983040 | tf_op jit(solution)/shard_map/slice | solution.py:13
  11.2 5.1 %collective-permute-start.2 = (f32[2,12,1024]{2,1,0:T(8,128)S(1)}, f32[2,12,1024]{2,1,0:T(8,128)S(1)}, u32[]{:S(2)}, u32[]{:S(2)}) collective-permute-start(f32[2,12,1024]{2,1,0:T(8,128)S(1)} %get-tuple-element.10), channel_id=1, source_target_pairs={{0,1},{1,2},{2,3},{3,4},{4,5},{5,6},{6,7},{8,9},{9,10},{10,11},{11... | collective-permute-start | bytes 294920 | tf_op jit(solution)/shard_map/ppermute | solution.py:12
  16.3 1.9 %collective-permute-start.3 = (f32[2,12,1024]{2,1,0:T(8,128)S(1)}, f32[2,12,1024]{2,1,0:T(8,128)S(1)}, u32[]{:S(2)}, u32[]{:S(2)}) collective-permute-start(f32[2,12,1024]{2,1,0:T(8,128)S(1)} %get-tuple-element.11), channel_id=1, source_target_pairs={{1,0},{2,1},{3,2},{4,3},{5,4},{6,5},{7,6},{9,8},{10,9},{11,10},{12... | collective-permute-start | bytes 294920 | tf_op jit(solution)/shard_map/ppermute | solution.py:15
  18.3 0.6 fusion.40
  18.9 3.7 %collective-permute-done.3 = f32[2,12,1024]{2,1,0:T(8,128)S(1)} collective-permute-done((f32[2,12,1024]{2,1,0:T(8,128)S(1)}, f32[2,12,1024]{2,1,0:T(8,128)S(1)}, u32[]{:S(2)}, u32[]{:S(2)}) %collective-permute-start.3) | collective-permute-done | bytes 98336 | tf_op jit(solution)/shard_map/ppermute | solution.py:15
  22.6 0.8 select_maximum_fusion
  23.6 0.4 fusion.1
  24.0 0.7 fusion.10
  24.7 0.7 fusion.6
  25.4 0.4 fusion.15
  25.8 0.7 fusion.8
  26.5 1.1 %fusion.36 = (f32[16,1024]{1,0:T(8,128)S(1)}, f32[16,8,1024]{2,1,0:T(8,128)}) fusion(f32[18,10,1024]{2,1,0:T(8,128)S(1)} %fusion.10, f32[]{:T(128)} %bitcast.26), kind=kLoop, calls=%fused_computation.91 | loop fusion | flops 1163264 | bytes 1114116 | tf_op jit(solution)/shard_map/reduce_sum | solution.py:71
  27.9 0.3 fusion.16
  28.1 2.3 %reduce_window_sum.11 = f32[16,8,1024]{2,1,0:T(8,128)} reduce-window(f32[16,8,1024]{2,1,0:T(8,128)} %get-tuple-element.9, f32[]{:T(128)} %constant.16.clone.1), window={size=1x8x1 pad=0_0x7_0x0_0}, to_apply=%region_0.1 | reduce-window | flops 917504 | bytes 1048580 | tf_op jit(solution)/shard_map/jit(cumsum)/reduce_window_sum | solution.py:59
  30.4 8.3 %multiply_reduce_fusion.3 = (f32[16,1024]{1,0:T(8,128)S(1)}, f32[16,1024]{1,0:T(8,128)S(1)}, f32[16,1024]{1,0:T(8,128)S(1)}) fusion(f32[18,10,1024]{2,1,0:T(8,128)S(1)} %fusion.10, f32[]{:T(128)} %bitcast.5, f32[]{:T(128)} %bitcast.4, f32[]{:T(128)} %bitcast.11, f32[]{:T(128)} %bitcast.10, f32[]{:T(128)} %bitcast.8, f32[]{:T(128)} %bitcast.7, f32[]{:T(128)} %bitcast.3, ...), kind=kLoop, calls=%fused_computation.79 | loop fusion | flops 6897664 | bytes 6488100 | tf_op jit(solution)/shard_map/reduce_sum | solution.py:63
  38.8 0.8 copy.12
  39.6 1.5 %bitcast_bitcast_fusion = f32[1024,1,4,16]{3,2,1,0:T(4,128)} fusion(f32[4,16,1024]{1,0,2:T(4,128)S(1)} %copy.12), kind=kLoop, calls=%fused_computation.95 | loop fusion | bytes 524288
  41.1 3.2 %reshape.83 = f32[64,1,1024]{2,1,0:T(1,128)S(1)} reshape(f32[1024,1,4,16]{3,2,1,0:T(4,128)} %bitcast_bitcast_fusion) | data formatting | bytes 524288
  44.3 30.7 %all_to_all.4 = f32[64,1,1024]{2,1,0:T(1,128)S(1)} all-to-all(f32[64,1,1024]{2,1,0:T(1,128)S(1)} %reshape.83), channel_id=1, replica_groups=mesh['depth'=64,'strip'=8] {'depth'}, dimensions={0} | all-to-all | bytes 524288 | tf_op jit(solution)/shard_map/all_to_all | solution.py:89
  75.0 0.5 broadcast.177
  75.5 1.3 %reduce = f32[64,1024]{1,0:T(8,128)S(1)} reduce(f32[64,1,1024]{2,1,0:T(1,128)S(1)} %all_to_all.4, f32[]{:T(128)} %broadcast.177), dimensions={1}, to_apply=%all_to_all.2.reduce_sub_computation | reduce | bytes 524292 | tf_op jit(solution)/shard_map/all_to_all | solution.py:89
  76.8 1.5 %reshape.84 = f32[1024,1,4,16]{3,2,1,0:T(4,128)S(1)} reshape(f32[64,1024]{1,0:T(8,128)S(1)} %reduce) | data formatting | bytes 524288
  78.3 0.5 slice.238
  79.0 6.3 %fusion.41 = f32[16,64,16]{2,0,1:T(8,128)S(1)} fusion(f32[16,64,16]{2,0,1:T(8,128)S(1)} %copy.14), kind=kOutput, calls=%fused_computation.96 | output fusion | flops 1032192 | bytes 131072 | tf_op jit(solution)/shard_map/jit(cumprod)/reduce_window | solution.py:92
  85.6 2.2 %copy.19 = f32[3,16,64,16]{3,2,1,0:T(8,128)} copy(f32[3,16,64,16]{1,0,3,2:T(4,128)S(1)} %bitcast.28) | data formatting | bytes 393216 | tf_op jit(solution)/shard_map/slice | solution.py:94
  87.9 1.7 %multiply_reduce_fusion = f32[3,16,16]{2,1,0:T(8,128)S(1)} fusion(f32[3,16,64,16]{3,2,1,0:T(8,128)} %copy.19, f32[16,64,16]{2,1,0:T(8,128)S(1)} %concatenate.18.clone), kind=kLoop, calls=%fused_computation.2 | loop fusion | flops 97536 | bytes 265216 | tf_op jit(solution)/shard_map/reduce_sum | solution.py:94
  89.6 0.6 pad_maximum_fusion.4
  (18 shorter events, 1.0 us)
Async XLA Ops:
  0.0 22.6 %copy-start = (f32[16,8,1024]{2,1,0:T(8,128)S(1)}, f32[16,8,1024]{2,1,0:T(8,128)}, u32[]{:S(2)}) copy-start(f32[16,8,1024]{2,1,0:T(8,128)} %param.4) | copy-start | bytes 1572868
  0.0 18.3 %copy-start.1 = (f32[3]{0:T(128)S(1)}, f32[3]{0:T(128)}, u32[]{:S(2)}) copy-start(f32[3]{0:T(128)} %param.7) | copy-start | bytes 40
  1.4 6.9 %collective-permute-start = (f32[16,2,1024]{2,1,0:T(2,128)S(1)}, f32[16,2,1024]{2,1,0:T(2,128)S(1)}, u32[]{:S(2)}, u32[]{:S(2)}) collective-permute-start(f32[16,2,1024]{2,1,0:T(2,128)S(1)} %get-tuple-element.12), channel_id=1, source_target_pairs={{0,8},{8,16},{16,24},{24,32},{32,40},{40,48},{48,56},{56,64},{64,7... | collective-permute-start | bytes 393224 | tf_op jit(solution)/shard_map/ppermute | solution.py:12
  4.6 5.7 %collective-permute-start.1 = (f32[16,2,1024]{2,1,0:T(2,128)S(1)}, f32[16,2,1024]{2,1,0:T(2,128)S(1)}, u32[]{:S(2)}, u32[]{:S(2)}) collective-permute-start(f32[16,2,1024]{2,1,0:T(2,128)S(1)} %get-tuple-element.13), channel_id=1, source_target_pairs={{8,0},{16,8},{24,16},{32,24},{40,32},{48,40},{56,48},{64,56},{72,6... | collective-permute-start | bytes 393224 | tf_op jit(solution)/shard_map/ppermute | solution.py:15
  11.2 7.7 %collective-permute-start.2 = (f32[2,12,1024]{2,1,0:T(8,128)S(1)}, f32[2,12,1024]{2,1,0:T(8,128)S(1)}, u32[]{:S(2)}, u32[]{:S(2)}) collective-permute-start(f32[2,12,1024]{2,1,0:T(8,128)S(1)} %get-tuple-element.10), channel_id=1, source_target_pairs={{0,1},{1,2},{2,3},{3,4},{4,5},{5,6},{6,7},{8,9},{9,10},{10,11},{11... | collective-permute-start | bytes 294920 | tf_op jit(solution)/shard_map/ppermute | solution.py:12
  16.3 6.3 %collective-permute-start.3 = (f32[2,12,1024]{2,1,0:T(8,128)S(1)}, f32[2,12,1024]{2,1,0:T(8,128)S(1)}, u32[]{:S(2)}, u32[]{:S(2)}) collective-permute-start(f32[2,12,1024]{2,1,0:T(8,128)S(1)} %get-tuple-element.11), channel_id=1, source_target_pairs={{1,0},{2,1},{3,2},{4,3},{5,4},{6,5},{7,6},{9,8},{10,9},{11,10},{12... | collective-permute-start | bytes 294920 | tf_op jit(solution)/shard_map/ppermute | solution.py:15
where the time goes:
time: 90.7 us; the launch traced here: 90.2 us
  blocking collectives  30.7 us (34%)
  other arithmetic  27 us (30%)
  local copies, waits for them, and re-layouts  14.3 us (16%)
  starting transfers between devices  11.5 us (13%)
  waiting for transfers between devices  5.76 us (6%)
    all_to_all x1, blocking collectives, local(): lax.all_to_all(partial_value[:, :, None, :], 'depth', split_axis=3, conca...  30.7 us
    reduce_sum x1, other arithmetic, render_slab(): jnp.sum(weights * jax.nn.sigmoid(color_map[channel, 0] * smoothed + color...  8.34 us
    ppermute x2, starting transfers between devices, extended_2(): lax.ppermute(lax.slice_in_dim(block, block.shape[dim] - width, None, axis...  8.32 us
    unnamed x8, local copies, waits for them, and re-layouts  6.35 us
    another operation x1, other arithmetic, local(): through = jnp.cumprod(layers[3], axis=1)  6.33 us
    ppermute x2, waiting for transfers between devices, extended_2(): lax.ppermute(lax.slice_in_dim(block, 0, width, axis=dim), axis, backward)  5.76 us
    ppermute x2, starting transfers between devices, extended_2(): lax.ppermute(lax.slice_in_dim(block, 0, width, axis=dim), axis, backward)  3.21 us
    another operation x1, other arithmetic, render_slab(): prior_depth = jnp.cumsum(optical, axis=1) - optical  2.28 us
  transfers between devices with their start and end apart: 4, of which 2 were waited for; matrix products, arithmetic and copies ran while one was open for 3% of the time, Pallas kernels for 0%

commit v1 on v0

--- a/solution.py
+++ b/solution.py
@@ -86,8 +86,14 @@
     smoothed = filtered[1:-1, 1:-1]
     gradient = gradients(pad_columns(filtered))
     partial_value = render_slab(smoothed, gradient, extinction, color_map, light_direction)
-    layers = lax.all_to_all(
-        partial_value[:, :, None, :], "depth", split_axis=3, concat_axis=2, tiled=True
+    layers = jnp.concatenate(
+        lax.all_to_all(
+            jnp.stack(jnp.split(partial_value[:, :, None, :], lax.axis_size("depth"), axis=3)),
+            "depth",
+            0,
+            0,
+        ),
+        axis=2,
     )
     through = jnp.cumprod(layers[3], axis=1)
     prior_pass = jnp.concatenate([jnp.ones_like(through[:, :1]), through[:, :-1]], 1)

time: 90.7 us -> 80.2 us (0.88)
  other arithmetic: 27 us -> 20.4 us
  local copies, waits for them, and re-layouts: 14.3 us -> 11.1 us
    another operation x1, other arithmetic: 6.33 us -> 0.07 us  [local(): through = jnp.cumprod(layers[3], axis=1)]
    slice x2 -> x0, local copies, waits for them, and re-layouts: 2.76 us -> none  [the longest x1 2.21 us: local(): colors = jnp.sum(prior_pass[None] * layers[:3], axis=2)]
    reduce_sum x1, other arithmetic: 1.7 us -> 0.27 us  [local(): colors = jnp.sum(prior_pass[None] * layers[:3], axis=2)]
    concatenate x1, other arithmetic: 0.76 us -> 1.84 us  [extended_2(): block = jnp.concatenate([low, block, high], axis=dim)]
    unnamed x8 -> x66, local copies, waits for them, and re-layouts: 6.35 us -> 5.87 us
  transfers between devices with their start and end apart: 4 -> 4, of which waited for: 2 -> 2; matrix products, arithmetic and copies ran while one was open for 3% -> 4% of each run, Pallas kernels for 0% -> 0%
where the time goes in v1:
time: 80.2 us; the launch traced here: 79.6 us
  blocking collectives  30.7 us (38%)
  other arithmetic  20.4 us (25%)
  starting transfers between devices  11.5 us (14%)
  local copies, waits for them, and re-layouts  11.1 us (14%)
  waiting for transfers between devices  5.01 us (6%)
  between operations  0.95 us (1%)
    all_to_all x1, blocking collectives, local(): lax.all_to_all(jnp.stack(jnp.split(partial_value[:, :, None, :], lax.axis...  30.7 us
    reduce_sum x1, other arithmetic, render_slab(): jnp.sum(weights * jax.nn.sigmoid(color_map[channel, 0] * smoothed + color...  8.34 us
    ppermute x2, starting transfers between devices, extended_2(): lax.ppermute(lax.slice_in_dim(block, block.shape[dim] - width, None, axis...  8.32 us
    unnamed x66, local copies, waits for them, and re-layouts  5.87 us
    ppermute x2, waiting for transfers between devices, extended_2(): lax.ppermute(lax.slice_in_dim(block, 0, width, axis=dim), axis, backward)  5 us
    ppermute x2, starting transfers between devices, extended_2(): lax.ppermute(lax.slice_in_dim(block, 0, width, axis=dim), axis, backward)  3.21 us
    another operation x1, other arithmetic, render_slab(): prior_depth = jnp.cumsum(optical, axis=1) - optical  2.28 us
    concatenate x1, other arithmetic, extended_2(): block = jnp.concatenate([low, block, high], axis=dim)  1.84 us
  transfers between devices with their start and end apart: 4, of which 2 were waited for; matrix products, arithmetic and copies ran while one was open for 4% of the time, Pallas kernels for 0%

profile of v1, /device:TPU:3, one launch (start us, length us, event | category | flops | bytes accessed | tf_op | source)
XLA Modules:
  0.0 79.6 jit_solution(1532458380561240820)
XLA Ops:
  0.0 1.4 %fusion.41 = (f32[16,2,1024]{2,1,0:T(2,128)S(1)}, f32[16,2,1024]{2,1,0:T(2,128)S(1)}) fusion(f32[16,8,1024]{2,1,0:T(8,128)} %param.4), kind=kLoop, calls=%fused_computation.224 | loop fusion | bytes 524288 | tf_op jit(solution)/shard_map/slice | solution.py:13
  1.4 3.2 %collective-permute-start = (f32[16,2,1024]{2,1,0:T(2,128)S(1)}, f32[16,2,1024]{2,1,0:T(2,128)S(1)}, u32[]{:S(2)}, u32[]{:S(2)}) collective-permute-start(f32[16,2,1024]{2,1,0:T(2,128)S(1)} %get-tuple-element.12), channel_id=1, source_target_pairs={{0,8},{8,16},{16,24},{24,32},{32,40},{40,48},{48,56},{56,64},{64,7... | collective-permute-start | bytes 393224 | tf_op jit(solution)/shard_map/ppermute | solution.py:12
  4.6 1.3 %collective-permute-start.1 = (f32[16,2,1024]{2,1,0:T(2,128)S(1)}, f32[16,2,1024]{2,1,0:T(2,128)S(1)}, u32[]{:S(2)}, u32[]{:S(2)}) collective-permute-start(f32[16,2,1024]{2,1,0:T(2,128)S(1)} %get-tuple-element.13), channel_id=1, source_target_pairs={{8,0},{16,8},{24,16},{32,24},{40,32},{48,40},{56,48},{64,56},{72,6... | collective-permute-start | bytes 393224 | tf_op jit(solution)/shard_map/ppermute | solution.py:15
  6.7 1.6 %fusion.42 = (f32[1,1]{0,1:T(1,128)}, f32[1,1]{0,1:T(1,128)}, f32[1,1]{0,1:T(1,128)}, f32[1,1]{0,1:T(1,128)}, f32[1,1]{0,1:T(1,128)}, /*index=5*/f32[1,1]{0,1:T(1,128)}) fusion(f32[3,2]{0,1:T(2,128)} %param.6), kind=kLoop, calls=%fused_computation.225 | loop fusion | bytes 48 | tf_op jit(solution)/shard_map/slice | solution.py:64
  8.3 2.1 %collective-permute-done.1 = f32[16,2,1024]{2,1,0:T(2,128)S(1)} collective-permute-done((f32[16,2,1024]{2,1,0:T(2,128)S(1)}, f32[16,2,1024]{2,1,0:T(2,128)S(1)}, u32[]{:S(2)}, u32[]{:S(2)}) %collective-permute-start.1) | collective-permute-done | bytes 131104 | tf_op jit(solution)/shard_map/ppermute | solution.py:15
  10.3 0.9 %pad_maximum_fusion.2 = (f32[2,12,1024]{2,1,0:T(8,128)S(1)}, f32[2,12,1024]{2,1,0:T(8,128)S(1)}) fusion(f32[16,2,1024]{2,1,0:T(2,128)S(1)} %collective-permute-done.1, f32[16,8,1024]{2,1,0:T(8,128)} %param.4, f32[16,2,1024]{2,1,0:T(2,128)S(1)} %collective-permute-done), kind=kLoop, calls=%fused_computation.151 | loop fusion | flops 98304 | bytes 983040 | tf_op jit(solution)/shard_map/slice | solution.py:13
  11.3 5.1 %collective-permute-start.2 = (f32[2,12,1024]{2,1,0:T(8,128)S(1)}, f32[2,12,1024]{2,1,0:T(8,128)S(1)}, u32[]{:S(2)}, u32[]{:S(2)}) collective-permute-start(f32[2,12,1024]{2,1,0:T(8,128)S(1)} %get-tuple-element.10), channel_id=1, source_target_pairs={{0,1},{1,2},{2,3},{3,4},{4,5},{5,6},{6,7},{8,9},{9,10},{10,11},{11... | collective-permute-start | bytes 294920 | tf_op jit(solution)/shard_map/ppermute | solution.py:12
  16.4 1.9 %collective-permute-start.3 = (f32[2,12,1024]{2,1,0:T(8,128)S(1)}, f32[2,12,1024]{2,1,0:T(8,128)S(1)}, u32[]{:S(2)}, u32[]{:S(2)}) collective-permute-start(f32[2,12,1024]{2,1,0:T(8,128)S(1)} %get-tuple-element.11), channel_id=1, source_target_pairs={{1,0},{2,1},{3,2},{4,3},{5,4},{6,5},{7,6},{9,8},{10,9},{11,10},{12... | collective-permute-start | bytes 294920 | tf_op jit(solution)/shard_map/ppermute | solution.py:15
  18.3 1.4 %fusion.43 = (f32[1]{0:T(128)}, f32[1]{0:T(128)}, f32[1]{0:T(128)}) fusion(f32[3]{0:T(128)} %param.7), kind=kLoop, calls=%fused_computation.226 | loop fusion | bytes 24 | tf_op jit(solution)/shard_map/slice | solution.py:52
  19.7 2.9 %collective-permute-done.3 = f32[2,12,1024]{2,1,0:T(8,128)S(1)} collective-permute-done((f32[2,12,1024]{2,1,0:T(8,128)S(1)}, f32[2,12,1024]{2,1,0:T(8,128)S(1)}, u32[]{:S(2)}, u32[]{:S(2)}) %collective-permute-start.3) | collective-permute-done | bytes 98336 | tf_op jit(solution)/shard_map/ppermute | solution.py:15
  22.7 1.8 %select_maximum_fusion = f32[20,12,1026]{2,1,0:T(8,128)S(1)} fusion(f32[2,12,1024]{2,1,0:T(8,128)S(1)} %collective-permute-done.3, f32[2,12,1024]{2,1,0:T(8,128)S(1)} %collective-permute-done.2, f32[16,2,1024]{2,1,0:T(2,128)S(1)} %collective-permute-done.1, f32[16,8,1024]{2,1,0:T(8,128)} %param.4, f32[16,2,1024]{2,1,0:T(2,128)S(1)} %collective-permute-done), kind=kLoop, calls=%fused_computation.6 | loop fusion | flops 2954880 | bytes 1968000 | tf_op jit(solution)/shard_map/concatenate | solution.py:16
  24.5 0.2 fusion.5
  24.7 0.4 fusion.3
  25.1 0.7 fusion.12
  25.8 0.7 fusion.8
  26.5 0.4 fusion.17
  26.9 0.7 fusion.10
  27.6 1.1 %fusion.39 = (f32[16,1024]{1,0:T(8,128)S(1)}, f32[16,8,1024]{2,1,0:T(8,128)}) fusion(f32[18,10,1024]{2,1,0:T(8,128)S(1)} %fusion.12, f32[]{:T(128)} %bitcast.292), kind=kLoop, calls=%fused_computation.223 | loop fusion | flops 1163264 | bytes 1114116 | tf_op jit(solution)/shard_map/reduce_sum | solution.py:71
  28.7 0.2 fusion.14
  29.0 0.3 fusion.18
  29.3 2.3 %reduce_window_sum.11 = f32[16,8,1024]{2,1,0:T(8,128)} reduce-window(f32[16,8,1024]{2,1,0:T(8,128)} %get-tuple-element.9, f32[]{:T(128)} %constant.16.clone.1), window={size=1x8x1 pad=0_0x7_0x0_0}, to_apply=%region_0.1 | reduce-window | flops 917504 | bytes 1048580 | tf_op jit(solution)/shard_map/jit(cumsum)/reduce_window_sum | solution.py:59
  31.5 8.3 %multiply_reduce_fusion.2 = (f32[16,1024]{1,0:T(8,128)S(1)}, f32[16,1024]{1,0:T(8,128)S(1)}, f32[16,1024]{1,0:T(8,128)S(1)}) fusion(f32[18,10,1024]{2,1,0:T(8,128)S(1)} %fusion.12, f32[]{:T(128)} %bitcast.5, f32[]{:T(128)} %bitcast.4, f32[]{:T(128)} %bitcast.11, f32[]{:T(128)} %bitcast.10, f32[]{:T(128)} %bitcast.8, f32[]{:T(128)} %bitcast.7, f32[]{:T(128)} %bitcast.3, ...), kind=kLoop, calls=%fused_computation.83 | loop fusion | flops 6897664 | bytes 6488100 | tf_op jit(solution)/shard_map/reduce_sum | solution.py:63
  40.7 0.1 constant_dynamic-update-slice_fusion.51
  44.3 0.1 bitcast_bitcast_fusion.1
  44.5 0.7 reshape.79
  45.2 30.7 %all_to_all.5 = f32[64,1,1024]{2,1,0:T(1,128)S(1)} all-to-all(f32[64,1,1024]{2,1,0:T(1,128)S(1)} %reshape.79), channel_id=1, replica_groups=mesh['depth'=64,'strip'=8] {'depth'}, dimensions={0} | all-to-all | bytes 524288 | tf_op jit(solution)/shard_map/all_to_all | solution.py:90
  75.9 0.5 broadcast.173
  76.4 1.3 %reduce = f32[64,1024]{1,0:T(8,128)S(1)} reduce(f32[64,1,1024]{2,1,0:T(1,128)S(1)} %all_to_all.5, f32[]{:T(128)} %broadcast.173), dimensions={1}, to_apply=%all_to_all.3.reduce_sub_computation | reduce | bytes 524292 | tf_op jit(solution)/shard_map/all_to_all | solution.py:90
  77.7 0.7 reshape.80
  78.4 0.1 bitcast_bitcast_fusion
  78.7 0.3 fusion.1
  79.0 0.6 pad_maximum_fusion.3
  (74 shorter events, 4.6 us)
Async XLA Ops:
  1.4 6.9 %collective-permute-start = (f32[16,2,1024]{2,1,0:T(2,128)S(1)}, f32[16,2,1024]{2,1,0:T(2,128)S(1)}, u32[]{:S(2)}, u32[]{:S(2)}) collective-permute-start(f32[16,2,1024]{2,1,0:T(2,128)S(1)} %get-tuple-element.12), channel_id=1, source_target_pairs={{0,8},{8,16},{16,24},{24,32},{32,40},{40,48},{48,56},{56,64},{64,7... | collective-permute-start | bytes 393224 | tf_op jit(solution)/shard_map/ppermute | solution.py:12
  4.6 5.7 %collective-permute-start.1 = (f32[16,2,1024]{2,1,0:T(2,128)S(1)}, f32[16,2,1024]{2,1,0:T(2,128)S(1)}, u32[]{:S(2)}, u32[]{:S(2)}) collective-permute-start(f32[16,2,1024]{2,1,0:T(2,128)S(1)} %get-tuple-element.13), channel_id=1, source_target_pairs={{8,0},{16,8},{24,16},{32,24},{40,32},{48,40},{56,48},{64,56},{72,6... | collective-permute-start | bytes 393224 | tf_op jit(solution)/shard_map/ppermute | solution.py:15
  11.3 8.5 %collective-permute-start.2 = (f32[2,12,1024]{2,1,0:T(8,128)S(1)}, f32[2,12,1024]{2,1,0:T(8,128)S(1)}, u32[]{:S(2)}, u32[]{:S(2)}) collective-permute-start(f32[2,12,1024]{2,1,0:T(8,128)S(1)} %get-tuple-element.10), channel_id=1, source_target_pairs={{0,1},{1,2},{2,3},{3,4},{4,5},{5,6},{6,7},{8,9},{9,10},{10,11},{11... | collective-permute-start | bytes 294920 | tf_op jit(solution)/shard_map/ppermute | solution.py:12
  16.4 6.3 %collective-permute-start.3 = (f32[2,12,1024]{2,1,0:T(8,128)S(1)}, f32[2,12,1024]{2,1,0:T(8,128)S(1)}, u32[]{:S(2)}, u32[]{:S(2)}) collective-permute-start(f32[2,12,1024]{2,1,0:T(8,128)S(1)} %get-tuple-element.11), channel_id=1, source_target_pairs={{1,0},{2,1},{3,2},{4,3},{5,4},{6,5},{7,6},{9,8},{10,9},{11,10},{12... | collective-permute-start | bytes 294920 | tf_op jit(solution)/shard_map/ppermute | solution.py:15
